TPU v7x, 256 devices: a whole 4x4x8 slice. The times are simulated.
256 devices in a mesh: sec: 4 (over x), px: 16 (over z, core), py: 4 (over y).
Axes of the slice: x: 4, y: 4, z: 8, core: 2. Of those that a mesh axis runs over, the one named last changes fastest.
Arguments:
- background: bfloat16 [2, 4, 512, 8192], P(None, 'sec', 'px', 'py'), may hold values from -6 to 6
- src_pos: int32 [16], replicated, may hold values from 0 to 1048575
- coupling: bfloat16 [4, 512, 512], P('sec', 'px'), may hold values from 0.3984375 to 1
- x_factor: bfloat16 [4, 2, 512, 512], P('sec', None, ('px', 'py')), may hold values from -1.25 to 1.25, as said below
- y_factor: bfloat16 [4, 2, 512, 512], P('sec', None, ('px', 'py')), may hold values from -1.25 to 1.25, as said below
Outputs:
- sweep_out: bfloat16 [2, 4, 512, 8192], P(None, 'sec', 'px', 'py')
Inputs may be any that keep to these rules, and one draw needn't show every extreme that they name: `x_factor`: factor entries; each is a dense complex matrix. `y_factor`: factor entries; each is a dense complex matrix.
All inputs are finite; a program needn't handle non-finite values.
Results may differ from a plain program's by a relative error of at most 0.02.
Values may be sent and summed in bfloat16 or wider, within the bound.
A program may use at most 64 MiB of HBM per device.

v0:
```python
import jax
import jax.numpy as jnp
from jax import lax
from jax.sharding import PartitionSpec as P

source_amplitude = 8.0


def shifted(x, axis, by):
    peers = lax.axis_size(axis)
    pairs = [(i, i + by) for i in range(peers) if 0 <= i + by < peers]
    return lax.ppermute(x, axis, pairs)


def complex_block(factor):
    upper = jnp.concatenate([factor[0], -factor[1]], axis=1)
    lower = jnp.concatenate([factor[1], factor[0]], axis=1)
    return jnp.concatenate([upper, lower], axis=0)


def y_transform(real_turned, imag_turned, field_in):
    planes, rows_here, merged = field_in.shape
    width = real_turned.shape[0]
    flat = field_in.reshape(planes, rows_here * merged // width, width)
    real_part = jnp.dot(flat[0], real_turned, preferred_element_type=jnp.float32) - jnp.dot(
        flat[1], imag_turned, preferred_element_type=jnp.float32
    )
    imag_part = jnp.dot(flat[0], imag_turned, preferred_element_type=jnp.float32) + jnp.dot(
        flat[1], real_turned, preferred_element_type=jnp.float32
    )
    return jnp.stack([real_part, imag_part]).astype(jnp.bfloat16).reshape(planes, rows_here, merged)


def x_transform(x_block, field_in):
    planes, rows_all, width = field_in.shape
    output = jnp.dot(
        x_block, field_in.reshape(planes * rows_all, width), preferred_element_type=jnp.float32
    )
    return output.astype(jnp.bfloat16).reshape(planes, rows_all, width)


def scale_rows(field_in, weights, width):
    planes, rows_here, merged = field_in.shape
    spread = field_in.astype(jnp.float32).reshape(planes, rows_here, merged // width, width)
    return (spread * weights.astype(jnp.float32)[None, :, None, :]).reshape(
        planes, rows_here, merged
    )


def on_device(background, src_pos, coupling, x_factor, y_factor):
    source_count = src_pos.shape[0]
    sec_count = lax.axis_size("sec")
    sec_index = lax.axis_index("sec")
    grid_y = lax.axis_size("py")
    own_x = lax.axis_index("px")
    own_y = lax.axis_index("py")
    local_sources = source_count // grid_y
    x_pieces, y_pieces = (
        lax.all_gather(x_factor[0], ("px", "py"), axis=1, tiled=True),
        lax.all_gather(y_factor[0], ("px", "py"), axis=1, tiled=True),
    )
    x_block = complex_block(x_pieces)
    real_turned = y_pieces[0].T
    imag_turned = y_pieces[1].T
    local_field = background[:, 0]
    local_weights = coupling[0]
    rows_here = local_field.shape[1]
    full_cols = y_factor.shape[3]
    plane_cells = x_factor.shape[3] * full_cols
    own_sources = lax.dynamic_slice_in_dim(src_pos, own_y * local_sources, local_sources)
    layer_of = own_sources // plane_cells
    remainder = own_sources % plane_cells
    row_of = remainder // full_cols
    column_of = remainder % full_cols
    row_start = own_x * rows_here
    row_hit = row_of[None, :] == row_start + jnp.arange(rows_here, dtype=jnp.int32)[:, None]
    col_hit = column_of[:, None] == jnp.arange(full_cols, dtype=jnp.int32)[None, :]
    layer_hit = layer_of == sec_index
    delta = (row_hit[:, :, None] & col_hit[None, :, :] & layer_hit[None, :, None]).astype(
        jnp.float32
    )
    delta = (delta * source_amplitude).reshape(rows_here, local_sources * full_cols)
    real_rhs = local_field[0].astype(jnp.float32) + delta
    rhs_field = jnp.stack([real_rhs, local_field[1].astype(jnp.float32)])

    def apply_front(field_in):
        turned = y_transform(real_turned, imag_turned, field_in)
        line_field = lax.all_to_all(turned, "px", split_axis=2, concat_axis=1, tiled=True)
        finished = x_transform(x_block, line_field)
        return lax.all_to_all(finished, "px", split_axis=1, concat_axis=2, tiled=True)

    forward_field = jnp.zeros(local_field.shape, jnp.bfloat16)
    for section in range(sec_count):
        incoming = shifted(forward_field, "sec", 1)
        reduced = (rhs_field - scale_rows(incoming, local_weights, full_cols)).astype(jnp.bfloat16)
        candidate = apply_front(reduced)
        forward_field = jnp.where(sec_index == section, candidate, forward_field)
    sweep_field = forward_field
    for section in range(sec_count - 2, -1, -1):
        sent_field = scale_rows(sweep_field, local_weights, full_cols).astype(jnp.bfloat16)
        incoming = shifted(sent_field, "sec", -1)
        solved = apply_front(incoming)
        candidate = (forward_field.astype(jnp.float32) - solved.astype(jnp.float32)).astype(
            jnp.bfloat16
        )
        sweep_field = jnp.where(sec_index == section, candidate, sweep_field)
    return sweep_field[:, None]


def solution(mesh):
    placed = (
        P(None, "sec", "px", "py"),
        P(),
        P("sec", "px", None),
        P("sec", None, ("px", "py"), None),
        P("sec", None, ("px", "py"), None),
    )
    return jax.shard_map(
        on_device, mesh=mesh, in_specs=placed, out_specs=P(None, "sec", "px", "py"), check_vma=False
    )
```

profile of v0, /device:TPU:136, one launch (start us, length us, event | category | flops | bytes accessed | tf_op | source)
XLA Modules:
  0.0 480.0 jit_solution(4595521641876577786)
XLA Ops:
  7.3 3.4 collective-permute-start
  13.8 2.5 collective-permute-done
  16.6 62.8 %all-gather.7.cloned.1.call-done = bf16[1,2,512,512]{3,2,1,0:T(8,128)(2,1)} async-done(((bf16[1,2,8,512]{3,2,1,0:T(8,128)(2,1)}), bf16[1,2,512,512]{3,2,1,0:T(8,128)(2,1)}) %all-gather.7.cloned.1.call-update) | async-done | bytes 1048592 | tf_op jit(solution)/shard_map/all_gather | solution.py:60
  83.7 1.7 reshape.512
  85.4 7.2 %all-to-all-start = ((bf16[16,2,4096]{2,1,0:T(2,128)(2,1)}), bf16[16,2,4096]{2,1,0:T(2,128)(2,1)S(1)}, u32[]{:S(2)}, u32[]{:S(2)}) async-start(bf16[16,2,4096]{2,1,0:T(2,128)(2,1)} %reshape.512), calls=%async_computation | async-start | bytes 524288 | tf_op jit(solution)/shard_map/all_to_all | solution.py:88
  92.7 58.8 %all-gather.5.cloned.1.call-done = bf16[1,2,512,512]{3,2,1,0:T(8,128)(2,1)} async-done(((bf16[1,2,8,512]{3,2,1,0:T(8,128)(2,1)}), bf16[1,2,512,512]{3,2,1,0:T(8,128)(2,1)}) %all-gather.5.cloned.1.call-update) | async-done | bytes 1048592 | tf_op jit(solution)/shard_map/all_gather | solution.py:59
  151.4 2.0 fusion.26
  155.0 1.8 copy.118
  156.8 2.2 convolution_convert_fusion.6
  159.9 7.2 %all-to-all-start.1 = ((bf16[2,512,128]{2,0,1:T(2,128)(2,1)}), bf16[2,512,128]{2,0,1:T(2,128)(2,1)S(1)}, u32[]{:S(2)}, u32[]{:S(2)}) async-start(bf16[2,512,128]{2,0,1:T(2,128)(2,1)} %copy.82), calls=%async_computation.1 | async-start | bytes 524288 | tf_op jit(solution)/shard_map/all_to_all | solution.py:90
  167.1 7.3 %all-to-all-done.1 = bf16[2,512,128]{2,0,1:T(2,128)(2,1)S(1)} async-done(((bf16[2,512,128]{2,0,1:T(2,128)(2,1)}), bf16[2,512,128]{2,0,1:T(2,128)(2,1)S(1)}, u32[]{:S(2)}, u32[]{:S(2)}) %all-to-all-start.1) | async-done | bytes 262176 | tf_op jit(solution)/shard_map/all_to_all | solution.py:90
  175.7 3.4 collective-permute-start.1
  179.1 5.8 %collective-permute-done.1 = bf16[2,32,2048]{2,1,0:T(8,128)(2,1)S(1)} collective-permute-done((bf16[2,32,2048]{2,1,0:T(8,128)(2,1)S(1)}, bf16[2,32,2048]{2,1,0:T(8,128)(2,1)S(1)}, u32[]{:S(2)}, u32[]{:S(2)}) %collective-permute-start.1) | collective-permute-done | bytes 262176 | tf_op jit(solution)/shard_map/ppermute | solution.py:12
  188.4 14.4 %all_to_all.195 = bf16[16,2,4096]{2,1,0:T(2,128)(2,1)S(1)} all-to-all(bf16[16,2,4096]{2,1,0:T(2,128)(2,1)S(1)} %reshape.514), channel_id=1, replica_groups=mesh['sec'=4,'px'=16,'py'=4] {'px'}, dimensions={0} | all-to-all | bytes 524288 | tf_op jit(solution)/shard_map/all_to_all | solution.py:88
  203.4 1.8 copy.120
  205.2 2.2 convolution_convert_fusion.5
  208.3 7.2 %all-to-all-start.3 = ((bf16[2,512,128]{2,0,1:T(2,128)(2,1)}), bf16[2,512,128]{2,0,1:T(2,128)(2,1)S(1)}, u32[]{:S(2)}, u32[]{:S(2)}) async-start(bf16[2,512,128]{2,0,1:T(2,128)(2,1)} %copy.87), calls=%async_computation.3 | async-start | bytes 524288 | tf_op jit(solution)/shard_map/all_to_all | solution.py:90
  215.5 7.3 %all-to-all-done.3 = bf16[2,512,128]{2,0,1:T(2,128)(2,1)S(1)} async-done(((bf16[2,512,128]{2,0,1:T(2,128)(2,1)}), bf16[2,512,128]{2,0,1:T(2,128)(2,1)S(1)}, u32[]{:S(2)}, u32[]{:S(2)}) %all-to-all-start.3) | async-done | bytes 262176 | tf_op jit(solution)/shard_map/all_to_all | solution.py:90
  223.2 4.6 collective-permute-start.2
  227.8 5.6 %collective-permute-done.2 = bf16[2,32,2048]{2,1,0:T(8,128)(2,1)S(1)} collective-permute-done((bf16[2,32,2048]{2,1,0:T(8,128)(2,1)S(1)}, bf16[2,32,2048]{2,1,0:T(8,128)(2,1)S(1)}, u32[]{:S(2)}, u32[]{:S(2)}) %collective-permute-start.2) | collective-permute-done | bytes 262176 | tf_op jit(solution)/shard_map/ppermute | solution.py:12
  237.0 14.4 %all_to_all.196 = bf16[16,2,4096]{2,1,0:T(2,128)(2,1)S(1)} all-to-all(bf16[16,2,4096]{2,1,0:T(2,128)(2,1)S(1)} %reshape.516), channel_id=1, replica_groups=mesh['sec'=4,'px'=16,'py'=4] {'px'}, dimensions={0} | all-to-all | bytes 524288 | tf_op jit(solution)/shard_map/all_to_all | solution.py:88
  251.9 1.8 copy.122
  253.6 2.2 convolution_convert_fusion.4
  256.8 7.2 %all-to-all-start.5 = ((bf16[2,512,128]{2,0,1:T(2,128)(2,1)}), bf16[2,512,128]{2,0,1:T(2,128)(2,1)S(1)}, u32[]{:S(2)}, u32[]{:S(2)}) async-start(bf16[2,512,128]{2,0,1:T(2,128)(2,1)} %copy.92), calls=%async_computation.5 | async-start | bytes 524288 | tf_op jit(solution)/shard_map/all_to_all | solution.py:90
  264.0 7.3 %all-to-all-done.5 = bf16[2,512,128]{2,0,1:T(2,128)(2,1)S(1)} async-done(((bf16[2,512,128]{2,0,1:T(2,128)(2,1)}), bf16[2,512,128]{2,0,1:T(2,128)(2,1)S(1)}, u32[]{:S(2)}, u32[]{:S(2)}) %all-to-all-start.5) | async-done | bytes 262176 | tf_op jit(solution)/shard_map/all_to_all | solution.py:90
  271.7 4.4 collective-permute-start.3
  276.1 5.8 %collective-permute-done.3 = bf16[2,32,2048]{2,1,0:T(8,128)(2,1)S(1)} collective-permute-done((bf16[2,32,2048]{2,1,0:T(8,128)(2,1)S(1)}, bf16[2,32,2048]{2,1,0:T(8,128)(2,1)S(1)}, u32[]{:S(2)}, u32[]{:S(2)}) %collective-permute-start.3) | collective-permute-done | bytes 262176 | tf_op jit(solution)/shard_map/ppermute | solution.py:12
  285.5 14.4 %all_to_all.197 = bf16[16,2,4096]{2,1,0:T(2,128)(2,1)S(1)} all-to-all(bf16[16,2,4096]{2,1,0:T(2,128)(2,1)S(1)} %reshape.518), channel_id=1, replica_groups=mesh['sec'=4,'px'=16,'py'=4] {'px'}, dimensions={0} | all-to-all | bytes 524288 | tf_op jit(solution)/shard_map/all_to_all | solution.py:88
  301.4 2.1 convolution_convert_fusion.3
  304.4 7.2 %all-to-all-start.7 = ((bf16[2,512,128]{2,0,1:T(2,128)(2,1)}), bf16[2,512,128]{2,0,1:T(2,128)(2,1)S(1)}, u32[]{:S(2)}, u32[]{:S(2)}) async-start(bf16[2,512,128]{2,0,1:T(2,128)(2,1)} %copy.97), calls=%async_computation.7 | async-start | bytes 524288 | tf_op jit(solution)/shard_map/all_to_all | solution.py:90
  311.7 7.3 %all-to-all-done.7 = bf16[2,512,128]{2,0,1:T(2,128)(2,1)S(1)} async-done(((bf16[2,512,128]{2,0,1:T(2,128)(2,1)}), bf16[2,512,128]{2,0,1:T(2,128)(2,1)S(1)}, u32[]{:S(2)}, u32[]{:S(2)}) %all-to-all-start.7) | async-done | bytes 262176 | tf_op jit(solution)/shard_map/all_to_all | solution.py:90
  321.0 9.7 %collective-permute-done.4 = bf16[2,32,2048]{2,1,0:T(8,128)(2,1)S(1)} collective-permute-done((bf16[2,32,2048]{2,1,0:T(8,128)(2,1)S(1)}, bf16[2,32,2048]{2,1,0:T(8,128)(2,1)S(1)}, u32[]{:S(2)}, u32[]{:S(2)}) %collective-permute-start.4) | collective-permute-done | bytes 262176 | tf_op jit(solution)/shard_map/ppermute | solution.py:12
  334.1 14.4 %all_to_all.198 = bf16[16,2,4096]{2,1,0:T(2,128)(2,1)S(1)} all-to-all(bf16[16,2,4096]{2,1,0:T(2,128)(2,1)S(1)} %reshape.520), channel_id=1, replica_groups=mesh['sec'=4,'px'=16,'py'=4] {'px'}, dimensions={0} | all-to-all | bytes 524288 | tf_op jit(solution)/shard_map/all_to_all | solution.py:88
  350.1 2.1 convolution_convert_fusion.2
  352.5 14.4 %all_to_all.199 = bf16[2,512,128]{2,0,1:T(2,128)(2,1)S(1)} all-to-all(bf16[2,512,128]{2,0,1:T(2,128)(2,1)S(1)} %copy.103), channel_id=1, replica_groups=mesh['sec'=4,'px'=16,'py'=4] {'px'}, dimensions={1} | all-to-all | bytes 524288 | tf_op jit(solution)/shard_map/all_to_all | solution.py:90
  368.8 8.9 %collective-permute-done.5 = bf16[2,32,2048]{2,1,0:T(8,128)(2,1)S(1)} collective-permute-done((bf16[2,32,2048]{2,1,0:T(8,128)(2,1)S(1)}, bf16[2,32,2048]{2,1,0:T(8,128)(2,1)S(1)}, u32[]{:S(2)}, u32[]{:S(2)}) %collective-permute-start.5) | collective-permute-done | bytes 262176 | tf_op jit(solution)/shard_map/ppermute | solution.py:12
  380.2 2.2 copy.105
  382.4 1.7 reshape.522
  384.1 16.0 %all_to_all.200 = bf16[16,2,4096]{2,1,0:T(2,128)(2,1)} all-to-all(bf16[16,2,4096]{2,1,0:T(2,128)(2,1)} %reshape.522), channel_id=1, replica_groups=mesh['sec'=4,'px'=16,'py'=4] {'px'}, dimensions={0} | all-to-all | bytes 524288 | tf_op jit(solution)/shard_map/all_to_all | solution.py:88
  400.1 3.0 reshape.523
  403.1 1.8 copy.128
  404.9 2.3 convolution_convert_fusion.1
  407.5 14.4 %all_to_all.201 = bf16[2,512,128]{2,0,1:T(2,128)(2,1)S(1)} all-to-all(bf16[2,512,128]{2,0,1:T(2,128)(2,1)S(1)} %copy.108), channel_id=1, replica_groups=mesh['sec'=4,'px'=16,'py'=4] {'px'}, dimensions={1} | all-to-all | bytes 524288 | tf_op jit(solution)/shard_map/all_to_all | solution.py:90
  425.8 8.9 %collective-permute-done.6 = bf16[2,32,2048]{2,1,0:T(8,128)(2,1)S(1)} collective-permute-done((bf16[2,32,2048]{2,1,0:T(8,128)(2,1)S(1)}, bf16[2,32,2048]{2,1,0:T(8,128)(2,1)S(1)}, u32[]{:S(2)}, u32[]{:S(2)}) %collective-permute-start.6) | collective-permute-done | bytes 262176 | tf_op jit(solution)/shard_map/ppermute | solution.py:12
  438.1 14.4 %all_to_all.202 = bf16[16,2,4096]{2,1,0:T(2,128)(2,1)S(1)} all-to-all(bf16[16,2,4096]{2,1,0:T(2,128)(2,1)S(1)} %reshape.524), channel_id=1, replica_groups=mesh['sec'=4,'px'=16,'py'=4] {'px'}, dimensions={0} | all-to-all | bytes 524288 | tf_op jit(solution)/shard_map/all_to_all | solution.py:88
  454.2 1.9 convolution_convert_fusion
  457.1 7.2 %all-to-all-start.13 = ((bf16[2,512,128]{2,0,1:T(2,128)(2,1)}), bf16[2,512,128]{2,0,1:T(2,128)(2,1)S(1)}, u32[]{:S(2)}, u32[]{:S(2)}) async-start(bf16[2,512,128]{2,0,1:T(2,128)(2,1)} %copy.113), calls=%async_computation.13 | async-start | bytes 524288 | tf_op jit(solution)/shard_map/all_to_all | solution.py:90
  464.9 6.8 %all-to-all-done.13 = bf16[2,512,128]{2,0,1:T(2,128)(2,1)S(1)} async-done(((bf16[2,512,128]{2,0,1:T(2,128)(2,1)}), bf16[2,512,128]{2,0,1:T(2,128)(2,1)S(1)}, u32[]{:S(2)}, u32[]{:S(2)}) %all-to-all-start.13) | async-done | bytes 262176 | tf_op jit(solution)/shard_map/all_to_all | solution.py:90
  (206 shorter events, 51.9 us)
Async XLA Ops:
  6.5 7.1 %copy-start.23 = (bf16[2,1,32,2048]{3,2,1,0:T(8,128)(2,1)S(1)}, bf16[2,1,32,2048]{3,2,1,0:T(8,128)(2,1)}, u32[]{:S(2)}) copy-start(bf16[2,1,32,2048]{3,2,1,0:T(8,128)(2,1)} %param.5) | copy-start | bytes 786436
  6.5 72.8 %all-gather.7.cloned.1.call-start = ((), (), s32[]{:S(2)}) async-start(), calls=%async_computation.15 | async-start | bytes 1064960 | tf_op jit(solution)/shard_map/all_gather | solution.py:60
  7.3 144.2 %all-gather.5.cloned.1.call-start = ((), (), s32[]{:S(2)}) async-start(), calls=%async_computation.14 | async-start | bytes 1064960 | tf_op jit(solution)/shard_map/all_gather | solution.py:59
  7.3 8.9 %collective-permute-start = (bf16[2,32,2048]{2,1,0:T(8,128)(2,1)S(1)}, bf16[2,32,2048]{2,1,0:T(8,128)(2,1)S(1)}, u32[]{:S(2)}, u32[]{:S(2)}) collective-permute-start(bf16[2,32,2048]{2,1,0:T(8,128)(2,1)S(1)} %broadcast_in_dim.4), channel_id=1, source_target_pairs={{0,64},{64,128},{128,192},{1,65},{65,129},{129,193},{2,66},{66,130... | collective-permute-start | bytes 786440 | tf_op jit(solution)/shard_map/ppermute | solution.py:12
  79.3 2.9 copy-start
  85.4 69.0 %all-to-all-start = ((bf16[16,2,4096]{2,1,0:T(2,128)(2,1)}), bf16[16,2,4096]{2,1,0:T(2,128)(2,1)S(1)}, u32[]{:S(2)}, u32[]{:S(2)}) async-start(bf16[16,2,4096]{2,1,0:T(2,128)(2,1)} %reshape.512), calls=%async_computation | async-start | bytes 524288 | tf_op jit(solution)/shard_map/all_to_all | solution.py:88
  151.4 2.0 copy-start.3
  155.0 1.8 copy-start.16
  159.9 14.6 %all-to-all-start.1 = ((bf16[2,512,128]{2,0,1:T(2,128)(2,1)}), bf16[2,512,128]{2,0,1:T(2,128)(2,1)S(1)}, u32[]{:S(2)}, u32[]{:S(2)}) async-start(bf16[2,512,128]{2,0,1:T(2,128)(2,1)} %copy.82), calls=%async_computation.1 | async-start | bytes 524288 | tf_op jit(solution)/shard_map/all_to_all | solution.py:90
  174.7 0.7 copy-start.4
  175.7 9.4 %copy-start.12 = (bf16[2,32,2048]{2,1,0:T(8,128)(2,1)}, bf16[2,32,2048]{2,1,0:T(8,128)(2,1)S(1)}, u32[]{:S(2)}) copy-start(bf16[2,32,2048]{2,1,0:T(8,128)(2,1)S(1)} %select_n.191) | copy-start | bytes 786436
  175.7 9.2 %collective-permute-start.1 = (bf16[2,32,2048]{2,1,0:T(8,128)(2,1)S(1)}, bf16[2,32,2048]{2,1,0:T(8,128)(2,1)S(1)}, u32[]{:S(2)}, u32[]{:S(2)}) collective-permute-start(bf16[2,32,2048]{2,1,0:T(8,128)(2,1)S(1)} %select_n.191), channel_id=1, source_target_pairs={{0,64},{64,128},{128,192},{1,65},{65,129},{129,193},{2,66},{66,130... | collective-permute-start | bytes 786440 | tf_op jit(solution)/shard_map/ppermute | solution.py:12
  203.4 1.8 copy-start.17
  207.3 15.9 %copy-start.13 = (bf16[2,32,2048]{2,1,0:T(8,128)(2,1)S(1)}, bf16[2,32,2048]{2,1,0:T(8,128)(2,1)}, u32[]{:S(2)}) copy-start(bf16[2,32,2048]{2,1,0:T(8,128)(2,1)} %copy-done.12) | copy-start | bytes 786436
  208.3 14.6 %all-to-all-start.3 = ((bf16[2,512,128]{2,0,1:T(2,128)(2,1)}), bf16[2,512,128]{2,0,1:T(2,128)(2,1)S(1)}, u32[]{:S(2)}, u32[]{:S(2)}) async-start(bf16[2,512,128]{2,0,1:T(2,128)(2,1)} %copy.87), calls=%async_computation.3 | async-start | bytes 524288 | tf_op jit(solution)/shard_map/all_to_all | solution.py:90
  222.9 10.7 %copy-start.6 = (bf16[2,512,128]{2,0,1:T(2,128)(2,1)}, bf16[2,512,128]{2,0,1:T(2,128)(2,1)S(1)}, u32[]{:S(2)}) copy-start(bf16[2,512,128]{2,0,1:T(2,128)(2,1)S(1)} %all-to-all-done.3) | copy-start | bytes 786436
  223.2 10.4 %copy-start.14 = (bf16[2,32,2048]{2,1,0:T(8,128)(2,1)}, bf16[2,32,2048]{2,1,0:T(8,128)(2,1)S(1)}, u32[]{:S(2)}) copy-start(bf16[2,32,2048]{2,1,0:T(8,128)(2,1)S(1)} %broadcast_select_fusion.5) | copy-start | bytes 786436
  223.2 10.2 %collective-permute-start.2 = (bf16[2,32,2048]{2,1,0:T(8,128)(2,1)S(1)}, bf16[2,32,2048]{2,1,0:T(8,128)(2,1)S(1)}, u32[]{:S(2)}, u32[]{:S(2)}) collective-permute-start(bf16[2,32,2048]{2,1,0:T(8,128)(2,1)S(1)} %broadcast_select_fusion.5), channel_id=1, source_target_pairs={{0,64},{64,128},{128,192},{1,65},{65,129},{129,193},{2,66},{66,130... | collective-permute-start | bytes 786440 | tf_op jit(solution)/shard_map/ppermute | solution.py:12
  251.9 1.8 copy-start.18
  255.8 15.9 %copy-start.15 = (bf16[2,32,2048]{2,1,0:T(8,128)(2,1)S(1)}, bf16[2,32,2048]{2,1,0:T(8,128)(2,1)}, u32[]{:S(2)}) copy-start(bf16[2,32,2048]{2,1,0:T(8,128)(2,1)} %copy-done.14) | copy-start | bytes 786436
  256.8 14.6 %all-to-all-start.5 = ((bf16[2,512,128]{2,0,1:T(2,128)(2,1)}), bf16[2,512,128]{2,0,1:T(2,128)(2,1)S(1)}, u32[]{:S(2)}, u32[]{:S(2)}) async-start(bf16[2,512,128]{2,0,1:T(2,128)(2,1)} %copy.92), calls=%async_computation.5 | async-start | bytes 524288 | tf_op jit(solution)/shard_map/all_to_all | solution.py:90
  271.4 10.6 %copy-start.8 = (bf16[2,512,128]{2,0,1:T(2,128)(2,1)}, bf16[2,512,128]{2,0,1:T(2,128)(2,1)S(1)}, u32[]{:S(2)}) copy-start(bf16[2,512,128]{2,0,1:T(2,128)(2,1)S(1)} %all-to-all-done.5) | copy-start | bytes 786436
  271.7 10.2 %collective-permute-start.3 = (bf16[2,32,2048]{2,1,0:T(8,128)(2,1)S(1)}, bf16[2,32,2048]{2,1,0:T(8,128)(2,1)S(1)}, u32[]{:S(2)}, u32[]{:S(2)}) collective-permute-start(bf16[2,32,2048]{2,1,0:T(8,128)(2,1)S(1)} %broadcast_select_fusion.6), channel_id=1, source_target_pairs={{0,64},{64,128},{128,192},{1,65},{65,129},{129,193},{2,66},{66,130... | collective-permute-start | bytes 786440 | tf_op jit(solution)/shard_map/ppermute | solution.py:12
  300.3 1.0 copy-start.19
  304.4 14.6 %all-to-all-start.7 = ((bf16[2,512,128]{2,0,1:T(2,128)(2,1)}), bf16[2,512,128]{2,0,1:T(2,128)(2,1)S(1)}, u32[]{:S(2)}, u32[]{:S(2)}) async-start(bf16[2,512,128]{2,0,1:T(2,128)(2,1)} %copy.97), calls=%async_computation.7 | async-start | bytes 524288 | tf_op jit(solution)/shard_map/all_to_all | solution.py:90
  319.0 0.7 copy-start.10
  319.7 47.7 %copy-start.1 = (bf16[2,32,2048]{2,1,0:T(8,128)(2,1)}, bf16[2,32,2048]{2,1,0:T(8,128)(2,1)S(1)}, u32[]{:S(2)}) copy-start(bf16[2,32,2048]{2,1,0:T(8,128)(2,1)S(1)} %get-tuple-element.6) | copy-start | bytes 786436
  319.7 11.0 %collective-permute-start.4 = (bf16[2,32,2048]{2,1,0:T(8,128)(2,1)S(1)}, bf16[2,32,2048]{2,1,0:T(8,128)(2,1)S(1)}, u32[]{:S(2)}, u32[]{:S(2)}) collective-permute-start(bf16[2,32,2048]{2,1,0:T(8,128)(2,1)S(1)} %get-tuple-element.5), channel_id=1, source_target_pairs={{64,0},{128,64},{192,128},{65,1},{129,65},{193,129},{66,2},{130,66... | collective-permute-start | bytes 786440 | tf_op jit(solution)/shard_map/ppermute | solution.py:12
  349.0 1.0 copy-start.20
  367.5 10.2 %collective-permute-start.5 = (bf16[2,32,2048]{2,1,0:T(8,128)(2,1)S(1)}, bf16[2,32,2048]{2,1,0:T(8,128)(2,1)S(1)}, u32[]{:S(2)}, u32[]{:S(2)}) collective-permute-start(bf16[2,32,2048]{2,1,0:T(8,128)(2,1)S(1)} %multiply_convert_fusion.1), channel_id=1, source_target_pairs={{64,0},{128,64},{192,128},{65,1},{129,65},{193,129},{66,2},{130,66... | collective-permute-start | bytes 786440 | tf_op jit(solution)/shard_map/ppermute | solution.py:12
  422.1 1.2 copy-start.2
  424.5 10.2 %collective-permute-start.6 = (bf16[2,32,2048]{2,1,0:T(8,128)(2,1)S(1)}, bf16[2,32,2048]{2,1,0:T(8,128)(2,1)S(1)}, u32[]{:S(2)}, u32[]{:S(2)}) collective-permute-start(bf16[2,32,2048]{2,1,0:T(8,128)(2,1)S(1)} %multiply_convert_fusion), channel_id=1, source_target_pairs={{64,0},{128,64},{192,128},{65,1},{129,65},{193,129},{66,2},{130,66... | collective-permute-start | bytes 786440 | tf_op jit(solution)/shard_map/ppermute | solution.py:12
  452.6 1.2 copy-start.21
  453.1 1.1 copy-start.22
  456.1 8.2 %copy-start.5 = (bf16[2,512,128]{2,0,1:T(2,128)(2,1)S(1)}, bf16[2,512,128]{2,0,1:T(2,128)(2,1)}, u32[]{:S(2)}) copy-start(bf16[2,512,128]{2,0,1:T(2,128)(2,1)} %copy-done.4) | copy-start | bytes 786436
  456.1 8.2 %copy-start.7 = (bf16[2,512,128]{2,0,1:T(2,128)(2,1)S(1)}, bf16[2,512,128]{2,0,1:T(2,128)(2,1)}, u32[]{:S(2)}) copy-start(bf16[2,512,128]{2,0,1:T(2,128)(2,1)} %copy-done.6) | copy-start | bytes 786436
  456.1 8.2 %copy-start.9 = (bf16[2,512,128]{2,0,1:T(2,128)(2,1)S(1)}, bf16[2,512,128]{2,0,1:T(2,128)(2,1)}, u32[]{:S(2)}) copy-start(bf16[2,512,128]{2,0,1:T(2,128)(2,1)} %copy-done.8) | copy-start | bytes 786436
  456.1 8.2 %copy-start.11 = (bf16[2,512,128]{2,0,1:T(2,128)(2,1)S(1)}, bf16[2,512,128]{2,0,1:T(2,128)(2,1)}, u32[]{:S(2)}) copy-start(bf16[2,512,128]{2,0,1:T(2,128)(2,1)} %copy-done.10) | copy-start | bytes 786436
  457.1 14.6 %all-to-all-start.13 = ((bf16[2,512,128]{2,0,1:T(2,128)(2,1)}), bf16[2,512,128]{2,0,1:T(2,128)(2,1)S(1)}, u32[]{:S(2)}, u32[]{:S(2)}) async-start(bf16[2,512,128]{2,0,1:T(2,128)(2,1)} %copy.113), calls=%async_computation.13 | async-start | bytes 524288 | tf_op jit(solution)/shard_map/all_to_all | solution.py:90
Sparse Core Ops, SparseCore 0:
  9.9 69.3 all-gather.6
  81.9 69.4 all-gather.4
where the time goes:
time: 489 us; the launch traced here: 480 us
  waiting for transfers between devices  206 us (42%)
  blocking collectives  117 us (24%)
  starting transfers between devices  63.1 us (13%)
  local copies, waits for them, and re-layouts  45.5 us (9%)
  matrix products  25.6 us (5%)
  between operations  14.7 us (3%)
  other arithmetic  8.7 us (2%)
    all_to_all x6, blocking collectives, apply_front(): lax.all_to_all(turned, 'px', split_axis=2, concat_axis=1, tiled=True)  88 us
    all_gather x1, waiting for transfers between devices, on_device(): lax.all_gather(y_factor[0], ('px', 'py'), axis=1, tiled=True)  62.8 us
    all_gather x1, waiting for transfers between devices, on_device(): lax.all_gather(x_factor[0], ('px', 'py'), axis=1, tiled=True)  58.8 us
    ppermute x7, waiting for transfers between devices, shifted(): return lax.ppermute(x, axis, pairs)  47.3 us
    all_to_all x5, starting transfers between devices, apply_front(): lax.all_to_all(finished, 'px', split_axis=1, concat_axis=2, tiled=True)  36.2 us
    all_to_all x5, waiting for transfers between devices, apply_front(): lax.all_to_all(finished, 'px', split_axis=1, concat_axis=2, tiled=True)  36.1 us
    all_to_all x2, blocking collectives, apply_front(): lax.all_to_all(finished, 'px', split_axis=1, concat_axis=2, tiled=True)  28.7 us
    ppermute x7, starting transfers between devices, shifted(): return lax.ppermute(x, axis, pairs)  19.7 us
  transfers between devices with their start and end apart: 15, of which 14 were waited for; matrix products, arithmetic and copies ran while one was open for 3% of the time, Pallas kernels for 0%

commit v1 on v0

v1 whole, which is shorter than its diff:
```python
import jax
import jax.numpy as jnp
from jax import lax
from jax.experimental import pallas as pl
from jax.experimental.pallas import tpu as pltpu
from jax.sharding import PartitionSpec as P

MESH = pl.DeviceIdType.MESH
source_amplitude = 8.0
f32 = jnp.float32
bf16 = jnp.bfloat16


def consumer_z(q, j, chips):
    return lax.rem(2 * q + j, chips)


def sweep_kernel(
    dims, src_ref, bg_ref, cp_ref, xf_ref, yf_ref, out_ref,
    landing, relay, factor, field, weights, sent, turned,
    send_sem, direct_sem, relay_sem, via_sem, field_sem, weight_sem, out_send, out_sem,
):
    secs, columns, grid_y, size = dims
    chips = columns // 2
    rows = size // columns
    q = lax.axis_index("sec")
    p = lax.axis_index("px")
    j = lax.axis_index("py")
    block = p * grid_y + j
    consumers = secs * grid_y
    devices = secs * columns * grid_y

    my_z = consumer_z(q, j, chips)
    is_consumer = p == 2 * my_z
    up_z = lax.rem(my_z + 1, chips)
    down_z = lax.rem(my_z + chips - 1, chips)
    is_up = p == 2 * up_z + 1
    is_down = p == 2 * down_z + 1
    is_relay = is_up | is_down

    barrier = pltpu.get_barrier_semaphore()

    @pl.when(is_consumer | is_relay)
    def _():
        def tell(i, carry):
            a = i // (columns * grid_y)
            r = lax.rem(i, columns * grid_y)
            pl.semaphore_signal(
                barrier, inc=1, device_id=(a, r // grid_y, lax.rem(r, grid_y)), device_id_type=MESH
            )
            return carry

        lax.fori_loop(0, devices, tell, 0)

    def announce(a, carry):
        pl.semaphore_signal(
            barrier, inc=1, device_id=(a, 2 * consumer_z(a, j, chips), j), device_id_type=MESH
        )
        return carry

    lax.fori_loop(0, secs, announce, 0)

    @pl.when(is_consumer)
    def _():
        pl.semaphore_wait(barrier, 3 * consumers + secs * columns)

    @pl.when(jnp.logical_not(is_consumer))
    def _():
        pl.semaphore_wait(barrier, 3 * consumers)

    def push(src, dst, recv, device, is_self):
        @pl.when(is_self)
        def _():
            pltpu.make_async_copy(src, dst, recv).start()

        @pl.when(jnp.logical_not(is_self))
        def _():
            pltpu.make_async_remote_copy(
                src_ref=src, dst_ref=dst, send_sem=send_sem, recv_sem=recv,
                device_id=device, device_id_type=MESH,
            ).start()

    def spread(i, carry):
        a = i // grid_y
        b = lax.rem(i, grid_y)
        z = consumer_z(a, b, chips)
        here = (a == q) & (b == j)
        push(
            yf_ref.at[0], landing.at[q, pl.ds(2, 2), block], direct_sem.at[q],
            (a, 2 * z, b), here & is_consumer,
        )
        push(
            xf_ref.at[0, 0], relay.at[q, block], relay_sem.at[q],
            (a, 2 * lax.rem(z + 1, chips) + 1, b), here & is_up,
        )
        push(
            xf_ref.at[0, 1], relay.at[q, block], relay_sem.at[q],
            (a, 2 * lax.rem(z + chips - 1, chips) + 1, b), here & is_down,
        )
        return carry

    lax.fori_loop(0, consumers, spread, 0)
    for a in range(secs):
        z = consumer_z(a, j, chips)
        own = pl.ds(pl.multiple_of(p * rows, rows), rows)
        here = (a == q) & is_consumer
        push(
            bg_ref.at[:, 0, :, pl.ds(a * size, size)], field.at[q, :, own, :], field_sem.at[q],
            (a, 2 * z, j), here,
        )
        push(cp_ref.at[0], weights.at[q, own, :], weight_sem.at[q], (a, 2 * z, j), here)

    def await_bytes(ref, sem):
        pltpu.make_async_copy(ref, ref, sem).wait()

    @pl.when(is_relay)
    def _():
        part = jnp.where(is_up, 0, 1)

        def forward(layer, carry):
            await_bytes(relay.at[layer], relay_sem.at[layer])
            pltpu.make_async_remote_copy(
                src_ref=relay.at[layer], dst_ref=landing.at[layer, part], send_sem=out_send,
                recv_sem=via_sem.at[part, layer], device_id=(q, 2 * my_z, j), device_id_type=MESH,
            ).start()
            return carry

        lax.fori_loop(0, secs, forward, 0)
        await_bytes(relay, out_send)

    @pl.when(is_consumer)
    def _():
        position = src_ref[j * secs + q]
        layer_of = position // (size * size)
        inside = position - layer_of * (size * size)
        row_of = inside // size
        column_of = inside - row_of * size
        row_ids = lax.broadcasted_iota(jnp.int32, (size, 1), 0)
        column_ids = lax.broadcasted_iota(jnp.int32, (1, size), 1)

        def dot(a, b):
            return jnp.dot(a, b, preferred_element_type=f32)

        def dot_turned(a, b):
            return lax.dot_general(a, b, (((1,), (1,)), ((), ())), preferred_element_type=f32)

        def front(layer, source):
            vr = source[0]
            vi = source[1]
            yr = factor[layer, 2]
            yi = factor[layer, 3]
            turned[0] = (dot_turned(vr, yr) - dot_turned(vi, yi)).astype(bf16)
            turned[1] = (dot_turned(vr, yi) + dot_turned(vi, yr)).astype(bf16)
            xr = factor[layer, 0]
            xi = factor[layer, 1]
            real = dot(xr, turned[0]) - dot(xi, turned[1])
            yield 0, real
            yield 1, dot(xr, turned[1]) + dot(xi, turned[0])

        def gather_rows(layer, planes):
            def step(k, carry):
                for m in planes:
                    tile = jnp.concatenate([landing[layer, m, 4 * k + i] for i in range(4)], axis=0)
                    factor[layer, m, pl.ds(pl.multiple_of(k * 32, 32), 32), :] = tile
                return carry

            lax.fori_loop(0, size // 32, step, 0)

        def emit(layer):
            def one(k, carry):
                piece = field.at[layer, :, pl.ds(pl.multiple_of(k * rows, rows), rows), :]
                target = out_ref.at[:, 0, :, pl.ds(pl.multiple_of(q * size, size), size)]
                here = (layer == q) & (k == p)

                @pl.when(here)
                def _():
                    pltpu.make_async_copy(piece, target, out_sem).start()

                @pl.when(jnp.logical_not(here))
                def _():
                    pltpu.make_async_remote_copy(
                        src_ref=piece, dst_ref=target, send_sem=out_send, recv_sem=out_sem,
                        device_id=(layer, k, j), device_id_type=MESH,
                    ).start()

                return carry

            lax.fori_loop(0, columns, one, 0)

        def forward(layer, carry):
            await_bytes(field.at[layer], field_sem.at[layer])
            await_bytes(weights.at[layer], weight_sem.at[layer])
            strength = jnp.where(layer_of == layer, source_amplitude, 0.0).astype(f32)
            bump = jnp.where(row_ids == row_of, strength, 0.0) * jnp.where(
                column_ids == column_of, 1.0, 0.0
            )

            @pl.when(layer == 0)
            def _():
                sent[0] = (field[0, 0].astype(f32) + bump).astype(bf16)
                sent[1] = field[0, 1]

            @pl.when(layer > 0)
            def _():
                scale = weights[layer].astype(f32)
                before = jnp.maximum(layer - 1, 0)
                sent[0] = (
                    field[layer, 0].astype(f32) + bump - scale * field[before, 0].astype(f32)
                ).astype(bf16)
                sent[1] = (
                    field[layer, 1].astype(f32) - scale * field[before, 1].astype(f32)
                ).astype(bf16)

            await_bytes(landing.at[layer, pl.ds(2, 2)], direct_sem.at[layer])
            gather_rows(layer, (2, 3))
            await_bytes(landing.at[layer, 0], via_sem.at[0, layer])
            await_bytes(landing.at[layer, 1], via_sem.at[1, layer])
            gather_rows(layer, (0, 1))
            for plane, value in front(layer, sent):
                field[layer, plane] = value.astype(bf16)
            return carry

        lax.fori_loop(0, secs, forward, 0)
        emit(secs - 1)

        def backward(step, carry):
            layer = secs - 2 - step
            scale = weights[layer + 1].astype(f32)
            sent[0] = (scale * field[layer + 1, 0].astype(f32)).astype(bf16)
            sent[1] = (scale * field[layer + 1, 1].astype(f32)).astype(bf16)
            for plane, value in front(layer, sent):
                solved = value.astype(bf16).astype(f32)
                field[layer, plane] = (field[layer, plane].astype(f32) - solved).astype(bf16)
            emit(layer)
            return carry

        lax.fori_loop(0, secs - 1, backward, 0)
        await_bytes(field.at[pl.ds(0, secs - 1)], out_send)
        await_bytes(field.at[0, :, pl.ds(0, size - rows), :], out_send)

    def sent_out(factor_bytes, field_blocks):
        pass

    await_bytes(landing.at[0, 0, pl.ds(0, 60)], send_sem)

    @pl.when(is_consumer)
    def _():
        await_bytes(landing.at[0, 0, pl.ds(0, 2)], send_sem)
        await_bytes(field.at[0, :, pl.ds(0, rows * (secs - 1)), :], send_sem)
        await_bytes(weights.at[0, pl.ds(0, rows * (secs - 1)), :], send_sem)

    @pl.when(is_relay)
    def _():
        await_bytes(landing.at[0, 0, pl.ds(0, 3)], send_sem)

    @pl.when(jnp.logical_not(is_relay | is_consumer))
    def _():
        await_bytes(landing.at[0, 0, pl.ds(0, 4)], send_sem)

    @pl.when(jnp.logical_not(is_consumer))
    def _():
        await_bytes(field.at[0, :, pl.ds(0, rows * secs), :], send_sem)
        await_bytes(weights.at[0, pl.ds(0, rows * secs), :], send_sem)

    await_bytes(out_ref, out_sem)


def solution(mesh):
    secs = mesh.shape["sec"]
    columns = mesh.shape["px"]
    grid_y = mesh.shape["py"]

    def on_device(background, src_pos, coupling, x_factor, y_factor):
        size = x_factor.shape[3]
        blocks = columns * grid_y
        height = x_factor.shape[2]
        dims = (secs, columns, grid_y, size)

        def body(*refs):
            sweep_kernel(dims, *refs)

        any_spec = pl.BlockSpec(memory_space=pl.ANY)
        dma = pltpu.SemaphoreType.DMA
        return pl.pallas_call(
            body,
            out_shape=jax.ShapeDtypeStruct(background.shape, bf16),
            in_specs=[pl.BlockSpec(memory_space=pltpu.SMEM)] + [any_spec] * 4,
            out_specs=any_spec,
            scratch_shapes=[
                pltpu.VMEM((secs, 4, blocks, height, size), bf16),
                pltpu.VMEM((secs, blocks, height, size), bf16),
                pltpu.VMEM((secs, 4, size, size), bf16),
                pltpu.VMEM((secs, 2, size, size), bf16),
                pltpu.VMEM((secs, size, size), bf16),
                pltpu.VMEM((2, size, size), bf16),
                pltpu.VMEM((2, size, size), bf16),
                dma, dma((secs,)), dma((secs,)), dma((2, secs)), dma((secs,)), dma((secs,)),
                dma, dma,
            ],
            compiler_params=pltpu.CompilerParams(
                collective_id=0, has_side_effects=True, vmem_limit_bytes=60 * 2**20
            ),
            name="sweep",
        )(src_pos, background, coupling, x_factor, y_factor)

    placed = (
        P(None, "sec", "px", "py"),
        P(),
        P("sec", "px", None),
        P("sec", None, ("px", "py"), None),
        P("sec", None, ("px", "py"), None),
    )
    return jax.shard_map(
        on_device, mesh=mesh, in_specs=placed, out_specs=P(None, "sec", "px", "py"), check_vma=False
    )
```

time: 489 us -> 110 us (0.22)
  the two profiles are of different devices: /device:TPU:136 before, /device:TPU:1 now
where the time goes in v1:
time: 110 us
  Pallas kernels  108 us (98%)
  local copies, waits for them, and re-layouts  1.67 us (2%)
    pallas_call x1, Pallas kernels, on_device(): pl.pallas_call(body, out_shape=jax.ShapeDtypeStruct(background.shape, bf1...  108 us

profile of v1, /device:TPU:1, one launch (start us, length us, event | category | flops | bytes accessed | tf_op | source)
XLA Modules:
  0.0 110.0 jit_solution(14583908177902604486)
XLA Ops:
  0.0 108.3 %sweep.1 = bf16[2,1,32,2048]{3,2,1,0:T(8,128)(2,1)} custom-call(s32[16]{0:T(128)} %refs_0_.1, bf16[2,1,32,2048]{3,2,1,0:T(8,128)(2,1)} %refs_1_.1, bf16[1,32,512]{2,1,0:T(8,128)(2,1)} %refs_2_.1, bf16[1,2,8,512]{3,2,1,0:T(8,128)(2,1)} %refs_3_.1, bf16[1,2,8,512]{3,2,1,0:T(8,128)(2,1)} %refs_4_.1), custom_call_target="tpu_custom_call" | custom-call | tf_op jit(solution)/shard_map/sweep/pallas_call | solution.py:284
  108.3 1.7 %copy.7 = bf16[2,1,32,2048]{3,2,1,0:T(8,128)(2,1)} copy(bf16[2,1,32,2048]{3,2,1,0:T(8,128)(2,1)} %sweep.1) | data formatting | bytes 524288

commit v2 on v1

v2 whole, which is shorter than its diff:
```python
import jax
import jax.numpy as jnp
from jax import lax
from jax.experimental import pallas as pl
from jax.experimental.pallas import tpu as pltpu
from jax.sharding import PartitionSpec as P

MESH = pl.DeviceIdType.MESH
source_amplitude = 8.0
f32 = jnp.float32
bf16 = jnp.bfloat16


def sweep_kernel(
    dims, src_ref, bg_ref, cp_ref, xf_ref, yf_ref, out_ref,
    landing, stage, stage_w, factor, field, weights, sent, turned,
    block_send, swap_send, field_send, relay_send, out_send,
    block_sem, swap_sem, swap_w_sem, ring_sem, plane_sem, field_sem, weight_sem, out_sem,
):
    secs, columns, grid_y, size = dims
    rows = size // columns
    q = lax.axis_index("sec")
    p = lax.axis_index("px")
    j = lax.axis_index("py")
    group = p // grid_y
    inner = lax.rem(p, grid_y)
    is_consumer = p == 0
    is_relay = p == 1
    hub = (group, 1, j)
    is_own_hub = is_relay & (q == group)

    barrier = pltpu.get_barrier_semaphore()

    def greet(device):
        pl.semaphore_signal(barrier, inc=1, device_id=device, device_id_type=MESH)

    for step in range(1, secs):
        greet((lax.rem(q + step, secs), p, j))

    @pl.when(is_relay)
    def _():
        def tell(i, carry):
            greet((i // grid_y, q * grid_y + lax.rem(i, grid_y), j))
            return carry

        lax.fori_loop(0, secs * grid_y, tell, 0)
        for step in range(1, secs):
            greet((lax.rem(q + step, secs), 1, j))
        for step in range(1, grid_y):
            greet((q, 1, lax.rem(j + step, grid_y)))

    @pl.when(is_consumer)
    def _():
        def tell(i, carry):
            greet((q, i, j))
            return carry

        lax.fori_loop(0, columns, tell, 0)

    for a in range(secs):
        greet((a, 0, j))

    expected = secs + 1 + jnp.where(is_consumer, secs * columns, 0)
    expected = expected + jnp.where(is_relay, secs + grid_y - 2, 0)
    pl.semaphore_wait(barrier, expected)

    def await_bytes(ref, sem):
        pltpu.make_async_copy(ref, ref, sem).wait()

    def send(src, dst, send_sem, recv_sem, device):
        pltpu.make_async_remote_copy(
            src_ref=src, dst_ref=dst, send_sem=send_sem, recv_sem=recv_sem,
            device_id=device, device_id_type=MESH,
        ).start()

    def push(src, dst, send_sem, recv_sem, device, is_self):
        @pl.when(is_self)
        def _():
            pltpu.make_async_copy(src, dst, recv_sem).start()

        @pl.when(jnp.logical_not(is_self))
        def _():
            send(src, dst, send_sem, recv_sem, device)

    push(
        yf_ref.at[0], landing.at[q, pl.ds(2, 2), group, j, inner], block_send, block_sem.at[q],
        hub, is_own_hub,
    )
    push(
        xf_ref.at[0], landing.at[q, pl.ds(0, 2), group, j, inner], block_send, block_sem.at[q],
        hub, is_own_hub,
    )

    def source_block(a):
        return bg_ref.at[:, 0, :, pl.ds(pl.multiple_of(a * size, size), size)]

    for step in range(1, secs):
        a = lax.rem(q + step, secs)
        send(source_block(a), stage.at[q], swap_send, swap_sem.at[q], (a, p, j))

        @pl.when(q > 0)
        def _():
            send(cp_ref.at[0], stage_w.at[q], swap_send, swap_w_sem.at[q], (a, p, j))

    own = pl.ds(pl.multiple_of(p * rows, rows), rows)
    home = (q, 0, j)
    for layer in range(secs):

        @pl.when(q == layer)
        def _():
            push(
                source_block(q), field.at[layer, :, own, :], field_send, field_sem.at[layer],
                home, is_consumer,
            )
            if layer:
                push(
                    cp_ref.at[0], weights.at[layer, own, :], field_send, weight_sem.at[layer],
                    home, is_consumer,
                )

        @pl.when(q != layer)
        def _():
            await_bytes(stage.at[layer], swap_sem.at[layer])
            push(
                stage.at[layer], field.at[layer, :, own, :], field_send, field_sem.at[layer],
                home, is_consumer,
            )
            if layer:
                await_bytes(stage_w.at[layer], swap_w_sem.at[layer])
                push(
                    stage_w.at[layer], weights.at[layer, own, :], field_send, weight_sem.at[layer],
                    home, is_consumer,
                )

    @pl.when(is_relay)
    def _():
        xs = [lax.rem(q + step, secs) for step in range(secs)]
        ys = [lax.rem(j + step, grid_y) for step in range(grid_y)]
        first = pl.ds(0, 2)
        second = pl.ds(2, 2)

        def open_layer(layer):
            await_bytes(landing.at[layer, :, 0, 0], block_sem.at[layer])
            piece = landing.at[layer, second, q, j]
            for y in ys[1:]:
                send(piece, piece, relay_send, ring_sem.at[0, layer], (q, 1, y))
            piece = landing.at[layer, first, q, j]
            for x in xs[1:]:
                send(piece, piece, relay_send, ring_sem.at[1, layer], (x, 1, j))

        def share(layer):
            await_bytes(landing.at[layer, second, 0, pl.ds(0, grid_y - 1)], ring_sem.at[0, layer])
            piece = landing.at[layer, second, q]
            send(piece, piece, relay_send, ring_sem.at[2, layer], (xs[1], 1, j))
            send(piece, piece, relay_send, ring_sem.at[3, layer], (xs[-1], 1, j))
            await_bytes(landing.at[layer, first, pl.ds(0, secs - 1), 0], ring_sem.at[1, layer])
            piece = landing.at[layer, first, :, j]
            send(piece, piece, relay_send, ring_sem.at[4, layer], (q, 1, ys[1]))
            send(piece, piece, relay_send, ring_sem.at[5, layer], (q, 1, ys[-1]))

        def relay(layer):
            await_bytes(landing.at[layer, second, 0], ring_sem.at[2, layer])
            piece = landing.at[layer, 2, xs[-1]]
            send(piece, piece, relay_send, ring_sem.at[6, layer], (xs[1], 1, j))
            await_bytes(landing.at[layer, second, 0], ring_sem.at[3, layer])
            piece = landing.at[layer, 3, xs[1]]
            send(piece, piece, relay_send, ring_sem.at[7, layer], (xs[-1], 1, j))
            await_bytes(landing.at[layer, first, :, 0], ring_sem.at[4, layer])
            piece = landing.at[layer, 0, :, ys[-1]]
            send(piece, piece, relay_send, ring_sem.at[8, layer], (q, 1, ys[1]))
            await_bytes(landing.at[layer, first, :, 0], ring_sem.at[5, layer])
            piece = landing.at[layer, 1, :, ys[1]]
            send(piece, piece, relay_send, ring_sem.at[9, layer], (q, 1, ys[-1]))

        def close_layer(layer):
            await_bytes(landing.at[layer, 2, 0], ring_sem.at[6, layer])
            await_bytes(landing.at[layer, 3, 0], ring_sem.at[7, layer])
            piece = landing.at[layer, second]
            send(piece, piece, relay_send, plane_sem.at[1, layer], home)
            await_bytes(landing.at[layer, 0, :, 0], ring_sem.at[8, layer])
            await_bytes(landing.at[layer, 1, :, 0], ring_sem.at[9, layer])
            piece = landing.at[layer, first]
            send(piece, piece, relay_send, plane_sem.at[0, layer], home)

        for tick in range(secs + 3):
            if tick == 0:
                for layer in range(secs):
                    open_layer(layer)
            if tick < secs:
                share(tick)
            if 1 <= tick <= secs:
                relay(tick - 1)
            if 2 <= tick <= secs + 1:
                close_layer(tick - 2)
        for layer in range(secs):
            for step in range(1, secs):
                await_bytes(landing.at[layer, second, 0, 0], relay_send)
                await_bytes(landing.at[layer, first, 0, 0], relay_send)
            for side in range(2):
                await_bytes(landing.at[layer, second, 0], relay_send)
                await_bytes(landing.at[layer, first, :, 0], relay_send)
                await_bytes(landing.at[layer, 2, 0], relay_send)
                await_bytes(landing.at[layer, 0, :, 0], relay_send)
            await_bytes(landing.at[layer], relay_send)

    @pl.when(is_consumer)
    def _():
        position = src_ref[j * secs + q]
        layer_of = position // (size * size)
        inside = position - layer_of * (size * size)
        row_of = inside // size
        column_of = inside - row_of * size
        column_ids = lax.broadcasted_iota(jnp.int32, (1, size), 1)
        on_column = jnp.where(column_ids == column_of, 1.0, 0.0).astype(f32)

        def dot(a, b):
            return jnp.dot(a, b, preferred_element_type=f32)

        def dot_turned(a, b):
            return lax.dot_general(a, b, (((1,), (1,)), ((), ())), preferred_element_type=f32)

        def front(layer, source):
            vr = source[0]
            vi = source[1]
            yr = factor[layer, 2]
            yi = factor[layer, 3]
            turned[0] = (dot_turned(vr, yr) - dot_turned(vi, yi)).astype(bf16)
            turned[1] = (dot_turned(vr, yi) + dot_turned(vi, yr)).astype(bf16)
            xr = factor[layer, 0]
            xi = factor[layer, 1]
            real = dot(xr, turned[0]) - dot(xi, turned[1])
            yield 0, real
            yield 1, dot(xr, turned[1]) + dot(xi, turned[0])

        def gather_rows(layer, planes):
            def step(k, carry):
                outer = k // grid_y
                slot = lax.rem(k, grid_y)
                for m in planes:
                    tile = jnp.concatenate(
                        [landing[layer, m, outer, i, slot] for i in range(grid_y)], axis=0
                    )
                    factor[layer, m, pl.ds(pl.multiple_of(k * 32, 32), 32), :] = tile
                return carry

            lax.fori_loop(0, size // 32, step, 0)

        def emit(layer):
            def one(k, carry):
                piece = field.at[layer, :, pl.ds(pl.multiple_of(k * rows, rows), rows), :]
                target = out_ref.at[:, 0, :, pl.ds(pl.multiple_of(q * size, size), size)]
                here = (layer == q) & (k == p)

                @pl.when(here)
                def _():
                    pltpu.make_async_copy(piece, target, out_sem).start()

                @pl.when(jnp.logical_not(here))
                def _():
                    pltpu.make_async_remote_copy(
                        src_ref=piece, dst_ref=target, send_sem=out_send, recv_sem=out_sem,
                        device_id=(layer, k, j), device_id_type=MESH,
                    ).start()

                return carry

            lax.fori_loop(0, columns, one, 0)

        def forward(layer, carry):
            await_bytes(field.at[layer], field_sem.at[layer])
            strength = jnp.where(layer_of == layer, source_amplitude, 0.0).astype(f32)

            def reduce_rows(k, coupled):
                part = pl.ds(pl.multiple_of(k * 32, 32), 32)
                hit = lax.broadcasted_iota(jnp.int32, (32, 1), 0) == row_of - k * 32
                bump = jnp.where(hit, strength, 0.0) * on_column
                real = field[layer, 0, part, :].astype(f32) + bump
                imag = field[layer, 1, part, :].astype(f32)
                if coupled:
                    scale = weights[layer, part, :].astype(f32)
                    real = real - scale * field[layer - 1, 0, part, :].astype(f32)
                    imag = imag - scale * field[layer - 1, 1, part, :].astype(f32)
                sent[0, part, :] = real.astype(bf16)
                sent[1, part, :] = imag.astype(bf16)

            def sweep_rows(coupled):
                def step(k, carry):
                    reduce_rows(k, coupled)
                    return carry

                lax.fori_loop(0, size // 32, step, 0, unroll=2)

            @pl.when(layer == 0)
            def _():
                sweep_rows(False)

            @pl.when(layer > 0)
            def _():
                await_bytes(weights.at[layer], weight_sem.at[layer])
                sweep_rows(True)

            await_bytes(landing.at[layer, pl.ds(2, 2)], plane_sem.at[1, layer])
            gather_rows(layer, (2, 3))
            await_bytes(landing.at[layer, pl.ds(0, 2)], plane_sem.at[0, layer])
            gather_rows(layer, (0, 1))
            for plane, value in front(layer, sent):
                field[layer, plane] = value.astype(bf16)
            return carry

        lax.fori_loop(0, secs, forward, 0)
        emit(secs - 1)

        def backward(step, carry):
            layer = secs - 2 - step

            def couple_rows(k, carry):
                part = pl.ds(pl.multiple_of(k * 32, 32), 32)
                scale = weights[layer + 1, part, :].astype(f32)
                for m in range(2):
                    sent[m, part, :] = (scale * field[layer + 1, m, part, :].astype(f32)).astype(bf16)
                return carry

            lax.fori_loop(0, size // 32, couple_rows, 0, unroll=2)
            for plane, value in front(layer, sent):
                solved = value.astype(bf16).astype(f32)
                field[layer, plane] = (field[layer, plane].astype(f32) - solved).astype(bf16)
            emit(layer)
            return carry

        lax.fori_loop(0, secs - 1, backward, 0)
        await_bytes(field.at[pl.ds(0, secs - 1)], out_send)
        await_bytes(field.at[0, :, pl.ds(0, size - rows), :], out_send)

    @pl.when(jnp.logical_not(is_own_hub))
    def _():
        await_bytes(landing.at[0, :, 0, 0, 0], block_send)

    await_bytes(stage.at[pl.ds(0, secs - 1)], swap_send)

    @pl.when(q > 0)
    def _():
        await_bytes(stage_w.at[pl.ds(0, secs - 1)], swap_send)

    @pl.when(jnp.logical_not(is_consumer))
    def _():
        await_bytes(stage, field_send)
        await_bytes(stage_w.at[pl.ds(0, secs - 1)], field_send)

    await_bytes(out_ref, out_sem)


def solution(mesh):
    secs = mesh.shape["sec"]
    columns = mesh.shape["px"]
    grid_y = mesh.shape["py"]

    def on_device(background, src_pos, coupling, x_factor, y_factor):
        size = x_factor.shape[3]
        height = x_factor.shape[2]
        dims = (secs, columns, grid_y, size)

        def body(*refs):
            sweep_kernel(dims, *refs)

        any_spec = pl.BlockSpec(memory_space=pl.ANY)
        dma = pltpu.SemaphoreType.DMA
        return pl.pallas_call(
            body,
            out_shape=jax.ShapeDtypeStruct(background.shape, bf16),
            in_specs=[pl.BlockSpec(memory_space=pltpu.SMEM)] + [any_spec] * 4,
            out_specs=any_spec,
            scratch_shapes=[
                pltpu.VMEM((secs, 4, columns // grid_y, grid_y, grid_y, height, size), bf16),
                pltpu.VMEM((secs, 2, size // columns, size), bf16),
                pltpu.VMEM((secs, size // columns, size), bf16),
                pltpu.VMEM((secs, 4, size, size), bf16),
                pltpu.VMEM((secs, 2, size, size), bf16),
                pltpu.VMEM((secs, size, size), bf16),
                pltpu.VMEM((2, size, size), bf16),
                pltpu.VMEM((2, size, size), bf16),
                dma, dma, dma, dma, dma,
                dma((secs,)), dma((secs,)), dma((secs,)), dma((10, secs)), dma((2, secs)),
                dma((secs,)), dma((secs,)), dma,
            ],
            compiler_params=pltpu.CompilerParams(
                collective_id=0, has_side_effects=True, vmem_limit_bytes=60 * 2**20
            ),
            name="sweep",
        )(src_pos, background, coupling, x_factor, y_factor)

    placed = (
        P(None, "sec", "px", "py"),
        P(),
        P("sec", "px", None),
        P("sec", None, ("px", "py"), None),
        P("sec", None, ("px", "py"), None),
    )
    return jax.shard_map(
        on_device, mesh=mesh, in_specs=placed, out_specs=P(None, "sec", "px", "py"), check_vma=False
    )
```

time: 110 us -> 98.5 us (0.90)
  the two profiles are of different devices: /device:TPU:1 before, /device:TPU:136 now
where the time goes in v2:
time: 98.5 us; the launch traced here: 97 us
  Pallas kernels  95.3 us (97%)
  local copies, waits for them, and re-layouts  1.67 us (2%)
    pallas_call x1, Pallas kernels, on_device(): pl.pallas_call(body, out_shape=jax.ShapeDtypeStruct(background.shape, bf1...  95.3 us

profile of v2, /device:TPU:136, one launch (start us, length us, event | category | flops | bytes accessed | tf_op | source)
XLA Modules:
  0.0 97.0 jit_solution(10572031883284818973)
XLA Ops:
  0.0 95.3 %sweep.1 = bf16[2,1,32,2048]{3,2,1,0:T(8,128)(2,1)} custom-call(s32[16]{0:T(128)} %refs_0_.1, bf16[2,1,32,2048]{3,2,1,0:T(8,128)(2,1)} %refs_1_.1, bf16[1,32,512]{2,1,0:T(8,128)(2,1)} %refs_2_.1, bf16[1,2,8,512]{3,2,1,0:T(8,128)(2,1)} %refs_3_.1, bf16[1,2,8,512]{3,2,1,0:T(8,128)(2,1)} %refs_4_.1), custom_call_target="tpu_custom_call" | custom-call | tf_op jit(solution)/shard_map/sweep/pallas_call | solution.py:367
  95.4 1.7 %copy.7 = bf16[2,1,32,2048]{3,2,1,0:T(8,128)(2,1)} copy(bf16[2,1,32,2048]{3,2,1,0:T(8,128)(2,1)} %sweep.1) | data formatting | bytes 524288

commit v3 on v2

--- a/solution.py
+++ b/solution.py
@@ -102,6 +102,14 @@
         def _():
             send(cp_ref.at[0], stage_w.at[q], swap_send, swap_w_sem.at[q], (a, p, j))
 
+    for layer in range(secs):
+
+        @pl.when(q != layer)
+        def _():
+            await_bytes(stage.at[layer], swap_sem.at[layer])
+            if layer:
+                await_bytes(stage_w.at[layer], swap_w_sem.at[layer])
+
     own = pl.ds(pl.multiple_of(p * rows, rows), rows)
     home = (q, 0, j)
     for layer in range(secs):
@@ -120,13 +128,11 @@
 
         @pl.when(q != layer)
         def _():
-            await_bytes(stage.at[layer], swap_sem.at[layer])
             push(
                 stage.at[layer], field.at[layer, :, own, :], field_send, field_sem.at[layer],
                 home, is_consumer,
             )
             if layer:
-                await_bytes(stage_w.at[layer], swap_w_sem.at[layer])
                 push(
                     stage_w.at[layer], weights.at[layer, own, :], field_send, weight_sem.at[layer],
                     home, is_consumer,

time: 98.5 us -> 82.2 us (0.83)
  Pallas kernels: 95.3 us -> 79.7 us
    pallas_call x1, Pallas kernels: 95.3 us -> 79.7 us  [on_device(): pl.pallas_call(body, out_shape=jax.ShapeDtypeStruct(background.shape, bf1...]
where the time goes in v3:
time: 82.2 us; the launch traced here: 81.4 us
  Pallas kernels  79.7 us (97%)
  local copies, waits for them, and re-layouts  1.67 us (2%)
    pallas_call x1, Pallas kernels, on_device(): pl.pallas_call(body, out_shape=jax.ShapeDtypeStruct(background.shape, bf1...  79.7 us
    unnamed x1, local copies, waits for them, and re-layouts  1.67 us

profile of v3, /device:TPU:136, one launch (start us, length us, event | category | flops | bytes accessed | tf_op | source)
XLA Modules:
  0.0 81.4 jit_solution(2947295578440074047)
XLA Ops:
  0.0 79.7 %sweep.1 = bf16[2,1,32,2048]{3,2,1,0:T(8,128)(2,1)} custom-call(s32[16]{0:T(128)} %refs_0_.1, bf16[2,1,32,2048]{3,2,1,0:T(8,128)(2,1)} %refs_1_.1, bf16[1,32,512]{2,1,0:T(8,128)(2,1)} %refs_2_.1, bf16[1,2,8,512]{3,2,1,0:T(8,128)(2,1)} %refs_3_.1, bf16[1,2,8,512]{3,2,1,0:T(8,128)(2,1)} %refs_4_.1), custom_call_target="tpu_custom_call" | custom-call | tf_op jit(solution)/shard_map/sweep/pallas_call | solution.py:373
  79.7 1.7 %copy.7 = bf16[2,1,32,2048]{3,2,1,0:T(8,128)(2,1)} copy(bf16[2,1,32,2048]{3,2,1,0:T(8,128)(2,1)} %sweep.1) | data formatting | bytes 524288

commit v4 on v3

--- a/solution.py
+++ b/solution.py
@@ -16,6 +16,7 @@
     landing, stage, stage_w, factor, field, weights, sent, turned,
     block_send, swap_send, field_send, relay_send, out_send,
     block_sem, swap_sem, swap_w_sem, ring_sem, plane_sem, field_sem, weight_sem, out_sem,
+    hop, hop_w, hop_out, hop_send, hop_sem, hop_w_sem, hop_out_sem, go_sem,
 ):
     secs, columns, grid_y, size = dims
     rows = size // columns
@@ -27,6 +28,11 @@
     is_consumer = p == 0
     is_relay = p == 1
     hub = (group, 1, j)
+    quarter = columns // 4
+    is_near = ((p >= 2) & (p < 2 + quarter)) | (p >= columns - quarter)
+    detour = columns // 2 + 1
+    helper = columns // 2 - 1
+    out_helper = columns // 2 + 3
     is_own_hub = is_relay & (q == group)
 
     barrier = pltpu.get_barrier_semaphore()
@@ -60,8 +66,19 @@
     for a in range(secs):
         greet((a, 0, j))
 
+    @pl.when(p == helper)
+    def _():
+        greet((q, detour, j))
+
+    @pl.when(p == detour)
+    def _():
+        for a in range(secs):
+            greet((a, out_helper, j))
+
     expected = secs + 1 + jnp.where(is_consumer, secs * columns, 0)
     expected = expected + jnp.where(is_relay, secs + grid_y - 2, 0)
+    expected = expected + jnp.where(p == detour, 1, 0)
+    expected = expected + jnp.where(p == out_helper, secs, 0)
     pl.semaphore_wait(barrier, expected)
 
     def await_bytes(ref, sem):
@@ -91,15 +108,20 @@
         hub, is_own_hub,
     )
 
+    def source_block_of(ref, a):
+        return ref.at[:, 0, :, pl.ds(pl.multiple_of(a * size, size), size)]
+
     def source_block(a):
-        return bg_ref.at[:, 0, :, pl.ds(pl.multiple_of(a * size, size), size)]
+        return source_block_of(bg_ref, a)
 
     for step in range(1, secs):
         a = lax.rem(q + step, secs)
         send(source_block(a), stage.at[q], swap_send, swap_sem.at[q], (a, p, j))
 
-        @pl.when(q > 0)
-        def _():
+    @pl.when(q > 0)
+    def _():
+        for step in range(1, secs):
+            a = lax.rem(q + step, secs)
             send(cp_ref.at[0], stage_w.at[q], swap_send, swap_w_sem.at[q], (a, p, j))
 
     for layer in range(secs):
@@ -107,35 +129,78 @@
         @pl.when(q != layer)
         def _():
             await_bytes(stage.at[layer], swap_sem.at[layer])
-            if layer:
-                await_bytes(stage_w.at[layer], swap_w_sem.at[layer])
-
-    own = pl.ds(pl.multiple_of(p * rows, rows), rows)
+
     home = (q, 0, j)
-    for layer in range(secs):
-
-        @pl.when(q == layer)
+    half = jnp.where(is_near, 1, 0)
+
+    @pl.when(is_near)
+    def _():
+        pl.semaphore_wait(go_sem, 1)
+
+    def rows_of(k):
+        return pl.ds(pl.multiple_of(k * rows, rows), rows)
+
+    def pass_on(layer, block, block_w):
+        @pl.when(p == detour)
+        def _():
+            send(block, hop.at[layer], field_send.at[layer], hop_sem.at[layer], (q, helper, j))
+
+        @pl.when(p != detour)
         def _():
             push(
-                source_block(q), field.at[layer, :, own, :], field_send, field_sem.at[layer],
+                block, field.at[layer, :, rows_of(p), :], field_send.at[layer], field_sem.at[half, layer],
                 home, is_consumer,
             )
+
+        if layer:
+
+            @pl.when(q != layer)
+            def _():
+                await_bytes(stage_w.at[layer], swap_w_sem.at[layer])
+
+            @pl.when(p == detour)
+            def _():
+                send(block_w, hop_w.at[layer], field_send.at[layer], hop_w_sem.at[layer], (q, helper, j))
+
+            @pl.when(p != detour)
+            def _():
+                push(
+                    block_w, weights.at[layer, rows_of(p), :], field_send.at[layer],
+                    weight_sem.at[half, layer], home, is_consumer,
+                )
+
+    def await_sent(layer):
+        @pl.when(jnp.logical_not(is_consumer))
+        def _():
+            await_bytes(stage.at[layer], field_send.at[layer])
             if layer:
-                push(
-                    cp_ref.at[0], weights.at[layer, own, :], field_send, weight_sem.at[layer],
-                    home, is_consumer,
-                )
+                await_bytes(stage_w.at[layer], field_send.at[layer])
+
+    for layer in range(secs):
+        if layer >= 1:
+            await_sent(layer - 1)
+
+        @pl.when(q == layer)
+        def _():
+            pass_on(layer, source_block(q), cp_ref.at[0])
 
         @pl.when(q != layer)
         def _():
-            push(
-                stage.at[layer], field.at[layer, :, own, :], field_send, field_sem.at[layer],
-                home, is_consumer,
+            pass_on(layer, stage.at[layer], stage_w.at[layer])
+
+    @pl.when(p == helper)
+    def _():
+        for layer in range(secs):
+            await_bytes(hop.at[layer], hop_sem.at[layer])
+            send(
+                hop.at[layer], field.at[layer, :, pl.ds(detour * rows, rows), :], hop_send,
+                field_sem.at[0, layer], home,
             )
             if layer:
-                push(
-                    stage_w.at[layer], weights.at[layer, own, :], field_send, weight_sem.at[layer],
-                    home, is_consumer,
+                await_bytes(hop_w.at[layer], hop_w_sem.at[layer])
+                send(
+                    hop_w.at[layer], weights.at[layer, pl.ds(detour * rows, rows), :], hop_send,
+                    weight_sem.at[0, layer], home,
                 )
 
     @pl.when(is_relay)
@@ -144,6 +209,9 @@
         ys = [lax.rem(j + step, grid_y) for step in range(grid_y)]
         first = pl.ds(0, 2)
         second = pl.ds(2, 2)
+
+        def deliver(piece, part, layer):
+            send(piece, piece, relay_send, plane_sem.at[part, layer], home)
 
         def open_layer(layer):
             await_bytes(landing.at[layer, :, 0, 0], block_sem.at[layer])
@@ -159,34 +227,38 @@
             piece = landing.at[layer, second, q]
             send(piece, piece, relay_send, ring_sem.at[2, layer], (xs[1], 1, j))
             send(piece, piece, relay_send, ring_sem.at[3, layer], (xs[-1], 1, j))
+            deliver(piece, 1, layer)
             await_bytes(landing.at[layer, first, pl.ds(0, secs - 1), 0], ring_sem.at[1, layer])
             piece = landing.at[layer, first, :, j]
             send(piece, piece, relay_send, ring_sem.at[4, layer], (q, 1, ys[1]))
             send(piece, piece, relay_send, ring_sem.at[5, layer], (q, 1, ys[-1]))
+            deliver(piece, 0, layer)
 
         def relay(layer):
             await_bytes(landing.at[layer, second, 0], ring_sem.at[2, layer])
             piece = landing.at[layer, 2, xs[-1]]
             send(piece, piece, relay_send, ring_sem.at[6, layer], (xs[1], 1, j))
+            deliver(landing.at[layer, second, xs[-1]], 1, layer)
             await_bytes(landing.at[layer, second, 0], ring_sem.at[3, layer])
             piece = landing.at[layer, 3, xs[1]]
             send(piece, piece, relay_send, ring_sem.at[7, layer], (xs[-1], 1, j))
+            deliver(landing.at[layer, second, xs[1]], 1, layer)
             await_bytes(landing.at[layer, first, :, 0], ring_sem.at[4, layer])
             piece = landing.at[layer, 0, :, ys[-1]]
             send(piece, piece, relay_send, ring_sem.at[8, layer], (q, 1, ys[1]))
+            deliver(landing.at[layer, first, :, ys[-1]], 0, layer)
             await_bytes(landing.at[layer, first, :, 0], ring_sem.at[5, layer])
             piece = landing.at[layer, 1, :, ys[1]]
             send(piece, piece, relay_send, ring_sem.at[9, layer], (q, 1, ys[-1]))
+            deliver(landing.at[layer, first, :, ys[1]], 0, layer)
 
         def close_layer(layer):
             await_bytes(landing.at[layer, 2, 0], ring_sem.at[6, layer])
             await_bytes(landing.at[layer, 3, 0], ring_sem.at[7, layer])
-            piece = landing.at[layer, second]
-            send(piece, piece, relay_send, plane_sem.at[1, layer], home)
+            deliver(landing.at[layer, second, xs[2]], 1, layer)
             await_bytes(landing.at[layer, 0, :, 0], ring_sem.at[8, layer])
             await_bytes(landing.at[layer, 1, :, 0], ring_sem.at[9, layer])
-            piece = landing.at[layer, first]
-            send(piece, piece, relay_send, plane_sem.at[0, layer], home)
+            deliver(landing.at[layer, first, :, ys[2]], 0, layer)
 
         for tick in range(secs + 3):
             if tick == 0:
@@ -261,19 +333,42 @@
                 def _():
                     pltpu.make_async_copy(piece, target, out_sem).start()
 
-                @pl.when(jnp.logical_not(here))
+                @pl.when(jnp.logical_not(here) & (k != detour))
                 def _():
-                    pltpu.make_async_remote_copy(
-                        src_ref=piece, dst_ref=target, send_sem=out_send, recv_sem=out_sem,
-                        device_id=(layer, k, j), device_id_type=MESH,
-                    ).start()
+                    send(piece, target, out_send, out_sem, (layer, k, j))
+
+                @pl.when(k == detour)
+                def _():
+                    send(piece, hop_out.at[layer], out_send, hop_out_sem.at[layer], (q, out_helper, j))
 
                 return carry
 
             lax.fori_loop(0, columns, one, 0)
 
+        half_rows = pl.ds(0, size // 2)
+
+        def await_half(which, layer):
+            await_bytes(field.at[layer, :, half_rows, :], field_sem.at[which, layer])
+
+        def await_half_w(which, layer):
+            await_bytes(weights.at[layer, half_rows, :], weight_sem.at[which, layer])
+
+        for layer in range(1):
+            await_half(0, layer)
+            if layer:
+                await_half_w(0, layer)
+        for step in range(quarter):
+            for k in (2 + step, columns - 1 - step):
+                pl.semaphore_signal(go_sem, inc=1, device_id=(q, k, j), device_id_type=MESH)
+
         def forward(layer, carry):
-            await_bytes(field.at[layer], field_sem.at[layer])
+            await_half(1, layer)
+
+            @pl.when(layer > 0)
+            def _():
+                await_half(0, layer)
+                await_half_w(0, layer)
+
             strength = jnp.where(layer_of == layer, source_amplitude, 0.0).astype(f32)
 
             def reduce_rows(k, coupled):
@@ -302,7 +397,7 @@
 
             @pl.when(layer > 0)
             def _():
-                await_bytes(weights.at[layer], weight_sem.at[layer])
+                await_half_w(1, layer)
                 sweep_rows(True)
 
             await_bytes(landing.at[layer, pl.ds(2, 2)], plane_sem.at[1, layer])
@@ -337,6 +432,13 @@
         await_bytes(field.at[pl.ds(0, secs - 1)], out_send)
         await_bytes(field.at[0, :, pl.ds(0, size - rows), :], out_send)
 
+    @pl.when(p == out_helper)
+    def _():
+        for layer in range(secs - 1, -1, -1):
+            await_bytes(hop_out.at[layer], hop_out_sem.at[layer])
+            send(hop_out.at[layer], source_block_of(out_ref, q), hop_send, out_sem, (layer, detour, j))
+        await_bytes(hop_out, hop_send)
+
     @pl.when(jnp.logical_not(is_own_hub))
     def _():
         await_bytes(landing.at[0, :, 0, 0, 0], block_send)
@@ -347,10 +449,13 @@
     def _():
         await_bytes(stage_w.at[pl.ds(0, secs - 1)], swap_send)
 
-    @pl.when(jnp.logical_not(is_consumer))
-    def _():
-        await_bytes(stage, field_send)
-        await_bytes(stage_w.at[pl.ds(0, secs - 1)], field_send)
+    for layer in range(secs - 1, secs):
+        await_sent(layer)
+
+    @pl.when(p == helper)
+    def _():
+        await_bytes(hop, hop_send)
+        await_bytes(hop_w.at[pl.ds(0, secs - 1)], hop_send)
 
     await_bytes(out_ref, out_sem)
 
@@ -384,9 +489,13 @@
                 pltpu.VMEM((secs, size, size), bf16),
                 pltpu.VMEM((2, size, size), bf16),
                 pltpu.VMEM((2, size, size), bf16),
-                dma, dma, dma, dma, dma,
+                dma, dma, dma((secs,)), dma, dma,
                 dma((secs,)), dma((secs,)), dma((secs,)), dma((10, secs)), dma((2, secs)),
-                dma((secs,)), dma((secs,)), dma,
+                dma((2, secs)), dma((2, secs)), dma,
+                pltpu.VMEM((secs, 2, size // columns, size), bf16),
+                pltpu.VMEM((secs, size // columns, size), bf16),
+                pltpu.VMEM((secs, 2, size // columns, size), bf16),
+                dma, dma((secs,)), dma((secs,)), dma((secs,)), pltpu.SemaphoreType.REGULAR,
             ],
             compiler_params=pltpu.CompilerParams(
                 collective_id=0, has_side_effects=True, vmem_limit_bytes=60 * 2**20

time: 82.2 us -> 76.1 us (0.926)
  Pallas kernels: 79.7 us -> 74.4 us
    pallas_call x1, Pallas kernels: 79.7 us -> 74.4 us  [on_device(): pl.pallas_call(body, out_shape=jax.ShapeDtypeStruct(background.shape, bf1...]
where the time goes in v4:
time: 76.1 us; the launch traced here: 76 us
  Pallas kernels  74.4 us (98%)
  local copies, waits for them, and re-layouts  1.67 us (2%)
    pallas_call x1, Pallas kernels, on_device(): pl.pallas_call(body, out_shape=jax.ShapeDtypeStruct(background.shape, bf1...  74.4 us
    unnamed x1, local copies, waits for them, and re-layouts  1.67 us

profile of v4, /device:TPU:136, one launch (start us, length us, event | category | flops | bytes accessed | tf_op | source)
XLA Modules:
  0.0 76.0 jit_solution(13271741866561696614)
XLA Ops:
  0.0 74.4 %sweep.1 = bf16[2,1,32,2048]{3,2,1,0:T(8,128)(2,1)} custom-call(s32[16]{0:T(128)} %refs_0_.1, bf16[2,1,32,2048]{3,2,1,0:T(8,128)(2,1)} %refs_1_.1, bf16[1,32,512]{2,1,0:T(8,128)(2,1)} %refs_2_.1, bf16[1,2,8,512]{3,2,1,0:T(8,128)(2,1)} %refs_3_.1, bf16[1,2,8,512]{3,2,1,0:T(8,128)(2,1)} %refs_4_.1), custom_call_target="tpu_custom_call" | custom-call | tf_op jit(solution)/shard_map/sweep/pallas_call | solution.py:478
  74.4 1.7 %copy.7 = bf16[2,1,32,2048]{3,2,1,0:T(8,128)(2,1)} copy(bf16[2,1,32,2048]{3,2,1,0:T(8,128)(2,1)} %sweep.1) | data formatting | bytes 524288

commit v5 on v4

--- a/solution.py
+++ b/solution.py
@@ -133,10 +133,6 @@
     home = (q, 0, j)
     half = jnp.where(is_near, 1, 0)
 
-    @pl.when(is_near)
-    def _():
-        pl.semaphore_wait(go_sem, 1)
-
     def rows_of(k):
         return pl.ds(pl.multiple_of(k * rows, rows), rows)
 
@@ -177,8 +173,25 @@
                 await_bytes(stage_w.at[layer], field_send.at[layer])
 
     for layer in range(secs):
+
+        if layer:
+
+            @pl.when(is_near)
+            def _():
+                pl.semaphore_wait(go_sem, 1)
+
+        if layer >= 2:
+
+            @pl.when(jnp.logical_not(is_near))
+            def _():
+                await_sent(layer - 2)
+
         if layer >= 1:
-            await_sent(layer - 1)
+
+            @pl.when(is_near)
+            def _():
+                await_sent(layer - 1)
+
 
         @pl.when(q == layer)
         def _():
@@ -260,16 +273,22 @@
             await_bytes(landing.at[layer, 1, :, 0], ring_sem.at[9, layer])
             deliver(landing.at[layer, first, :, ys[2]], 0, layer)
 
-        for tick in range(secs + 3):
-            if tick == 0:
-                for layer in range(secs):
-                    open_layer(layer)
-            if tick < secs:
-                share(tick)
-            if 1 <= tick <= secs:
-                relay(tick - 1)
-            if 2 <= tick <= secs + 1:
-                close_layer(tick - 2)
+        open_layer(0)
+        open_layer(1)
+        share(0)
+        open_layer(2)
+        share(1)
+        open_layer(3)
+        relay(0)
+        share(2)
+        relay(1)
+        close_layer(0)
+        share(3)
+        relay(2)
+        close_layer(1)
+        relay(3)
+        close_layer(2)
+        close_layer(3)
         for layer in range(secs):
             for step in range(1, secs):
                 await_bytes(landing.at[layer, second, 0, 0], relay_send)
@@ -323,10 +342,10 @@
 
             lax.fori_loop(0, size // 32, step, 0)
 
-        def emit(layer):
+        def emit(layer, plane):
             def one(k, carry):
-                piece = field.at[layer, :, pl.ds(pl.multiple_of(k * rows, rows), rows), :]
-                target = out_ref.at[:, 0, :, pl.ds(pl.multiple_of(q * size, size), size)]
+                piece = field.at[layer, plane, pl.ds(pl.multiple_of(k * rows, rows), rows), :]
+                target = out_ref.at[plane, 0, :, pl.ds(pl.multiple_of(q * size, size), size)]
                 here = (layer == q) & (k == p)
 
                 @pl.when(here)
@@ -339,7 +358,7 @@
 
                 @pl.when(k == detour)
                 def _():
-                    send(piece, hop_out.at[layer], out_send, hop_out_sem.at[layer], (q, out_helper, j))
+                    send(piece, hop_out.at[layer, plane], out_send, hop_out_sem.at[layer], (q, out_helper, j))
 
                 return carry
 
@@ -353,21 +372,16 @@
         def await_half_w(which, layer):
             await_bytes(weights.at[layer, half_rows, :], weight_sem.at[which, layer])
 
-        for layer in range(1):
+        near_chips = [*range(2, 2 + quarter), *range(columns - quarter, columns)]
+        for layer in range(secs):
             await_half(0, layer)
             if layer:
                 await_half_w(0, layer)
-        for step in range(quarter):
-            for k in (2 + step, columns - 1 - step):
+            for k in () if layer == secs - 1 else near_chips:
                 pl.semaphore_signal(go_sem, inc=1, device_id=(q, k, j), device_id_type=MESH)
 
         def forward(layer, carry):
             await_half(1, layer)
-
-            @pl.when(layer > 0)
-            def _():
-                await_half(0, layer)
-                await_half_w(0, layer)
 
             strength = jnp.where(layer_of == layer, source_amplitude, 0.0).astype(f32)
 
@@ -406,10 +420,14 @@
             gather_rows(layer, (0, 1))
             for plane, value in front(layer, sent):
                 field[layer, plane] = value.astype(bf16)
+
+                @pl.when(layer == secs - 1)
+                def _():
+                    emit(layer, plane)
+
             return carry
 
         lax.fori_loop(0, secs, forward, 0)
-        emit(secs - 1)
 
         def backward(step, carry):
             layer = secs - 2 - step
@@ -425,7 +443,7 @@
             for plane, value in front(layer, sent):
                 solved = value.astype(bf16).astype(f32)
                 field[layer, plane] = (field[layer, plane].astype(f32) - solved).astype(bf16)
-            emit(layer)
+                emit(layer, plane)
             return carry
 
         lax.fori_loop(0, secs - 1, backward, 0)
@@ -449,8 +467,16 @@
     def _():
         await_bytes(stage_w.at[pl.ds(0, secs - 1)], swap_send)
 
-    for layer in range(secs - 1, secs):
-        await_sent(layer)
+    @pl.when(jnp.logical_not(is_near))
+    def _():
+        for layer in range(secs - 2, secs):
+            await_sent(layer)
+
+    @pl.when(is_near)
+    def _():
+        for layer in range(secs - 1, secs):
+            await_sent(layer)
+
 
     @pl.when(p == helper)
     def _():

time: 76.1 us -> 73.9 us (0.971)
  Pallas kernels: 74.4 us -> 72 us
    pallas_call x1, Pallas kernels: 74.4 us -> 72 us  [on_device(): pl.pallas_call(body, out_shape=jax.ShapeDtypeStruct(background.shape, bf1...]
where the time goes in v5:
time: 73.9 us; the launch traced here: 73.7 us
  Pallas kernels  72 us (97%)
  local copies, waits for them, and re-layouts  1.67 us (2%)
    pallas_call x1, Pallas kernels, on_device(): pl.pallas_call(body, out_shape=jax.ShapeDtypeStruct(background.shape, bf1...  72 us
    unnamed x1, local copies, waits for them, and re-layouts  1.67 us

profile of v5, /device:TPU:136, one launch (start us, length us, event | category | flops | bytes accessed | tf_op | source)
XLA Modules:
  0.0 73.7 jit_solution(5527667331168352995)
XLA Ops:
  0.0 72.0 %sweep.1 = bf16[2,1,32,2048]{3,2,1,0:T(8,128)(2,1)} custom-call(s32[16]{0:T(128)} %refs_0_.1, bf16[2,1,32,2048]{3,2,1,0:T(8,128)(2,1)} %refs_1_.1, bf16[1,32,512]{2,1,0:T(8,128)(2,1)} %refs_2_.1, bf16[1,2,8,512]{3,2,1,0:T(8,128)(2,1)} %refs_3_.1, bf16[1,2,8,512]{3,2,1,0:T(8,128)(2,1)} %refs_4_.1), custom_call_target="tpu_custom_call" | custom-call | tf_op jit(solution)/shard_map/sweep/pallas_call | solution.py:504
  72.0 1.7 %copy.7 = bf16[2,1,32,2048]{3,2,1,0:T(8,128)(2,1)} copy(bf16[2,1,32,2048]{3,2,1,0:T(8,128)(2,1)} %sweep.1) | data formatting | bytes 524288

commit v6 on v5

--- a/solution.py
+++ b/solution.py
@@ -40,16 +40,11 @@
     def greet(device):
         pl.semaphore_signal(barrier, inc=1, device_id=device, device_id_type=MESH)
 
-    for step in range(1, secs):
-        greet((lax.rem(q + step, secs), p, j))
-
     @pl.when(is_relay)
     def _():
-        def tell(i, carry):
-            greet((i // grid_y, q * grid_y + lax.rem(i, grid_y), j))
-            return carry
-
-        lax.fori_loop(0, secs * grid_y, tell, 0)
+        for a in (2, 1, 3, 0):
+            for b in range(grid_y):
+                greet((lax.rem(q + a, secs), q * grid_y + b, j))
         for step in range(1, secs):
             greet((lax.rem(q + step, secs), 1, j))
         for step in range(1, grid_y):
@@ -57,11 +52,11 @@
 
     @pl.when(is_consumer)
     def _():
-        def tell(i, carry):
-            greet((q, i, j))
-            return carry
-
-        lax.fori_loop(0, columns, tell, 0)
+        for b in range(columns):
+            greet((q, (b + columns // 4) % columns, j))
+
+    for step in range(1, secs):
+        greet((lax.rem(q + step, secs), p, j))
 
     for a in range(secs):
         greet((a, 0, j))
@@ -343,26 +338,15 @@
             lax.fori_loop(0, size // 32, step, 0)
 
         def emit(layer, plane):
-            def one(k, carry):
-                piece = field.at[layer, plane, pl.ds(pl.multiple_of(k * rows, rows), rows), :]
-                target = out_ref.at[plane, 0, :, pl.ds(pl.multiple_of(q * size, size), size)]
-                here = (layer == q) & (k == p)
-
-                @pl.when(here)
-                def _():
-                    pltpu.make_async_copy(piece, target, out_sem).start()
-
-                @pl.when(jnp.logical_not(here) & (k != detour))
-                def _():
+            target = out_ref.at[plane, 0, :, pl.ds(pl.multiple_of(q * size, size), size)]
+            for k in range(columns):
+                piece = field.at[layer, plane, pl.ds(k * rows, rows), :]
+                if k == 0:
+                    push(piece, target, out_send, out_sem, (layer, k, j), layer == q)
+                elif k == detour:
+                    send(piece, hop_out.at[layer, plane], out_send, hop_out_sem.at[layer], (q, out_helper, j))
+                else:
                     send(piece, target, out_send, out_sem, (layer, k, j))
-
-                @pl.when(k == detour)
-                def _():
-                    send(piece, hop_out.at[layer, plane], out_send, hop_out_sem.at[layer], (q, out_helper, j))
-
-                return carry
-
-            lax.fori_loop(0, columns, one, 0)
 
         half_rows = pl.ds(0, size // 2)
 
@@ -373,15 +357,22 @@
             await_bytes(weights.at[layer, half_rows, :], weight_sem.at[which, layer])
 
         near_chips = [*range(2, 2 + quarter), *range(columns - quarter, columns)]
-        for layer in range(secs):
+        for layer in range(3):
             await_half(0, layer)
             if layer:
                 await_half_w(0, layer)
-            for k in () if layer == secs - 1 else near_chips:
-                pl.semaphore_signal(go_sem, inc=1, device_id=(q, k, j), device_id_type=MESH)
+            waves = 0 if layer == secs - 1 else 1
+            for k in near_chips if waves else ():
+                pl.semaphore_signal(go_sem, inc=waves, device_id=(q, k, j), device_id_type=MESH)
 
         def forward(layer, carry):
             await_half(1, layer)
+
+            @pl.when(layer >= 3)
+            def _():
+                await_half(0, layer)
+                await_half_w(0, layer)
+
 
             strength = jnp.where(layer_of == layer, source_amplitude, 0.0).astype(f32)
 

time: 73.9 us -> 73.6 us (level)
  no operation moved by 1% of the time
where the time goes in v6:
time: 73.6 us; the launch traced here: 73.5 us
  Pallas kernels  71.8 us (98%)
  local copies, waits for them, and re-layouts  1.67 us (2%)
    pallas_call x1, Pallas kernels, on_device(): pl.pallas_call(body, out_shape=jax.ShapeDtypeStruct(background.shape, bf1...  71.8 us
    unnamed x1, local copies, waits for them, and re-layouts  1.67 us

profile of v6, /device:TPU:136, one launch (start us, length us, event | category | flops | bytes accessed | tf_op | source)
XLA Modules:
  0.0 73.5 jit_solution(7228574476839322277)
XLA Ops:
  0.0 71.8 %sweep.1 = bf16[2,1,32,2048]{3,2,1,0:T(8,128)(2,1)} custom-call(s32[16]{0:T(128)} %refs_0_.1, bf16[2,1,32,2048]{3,2,1,0:T(8,128)(2,1)} %refs_1_.1, bf16[1,32,512]{2,1,0:T(8,128)(2,1)} %refs_2_.1, bf16[1,2,8,512]{3,2,1,0:T(8,128)(2,1)} %refs_3_.1, bf16[1,2,8,512]{3,2,1,0:T(8,128)(2,1)} %refs_4_.1), custom_call_target="tpu_custom_call" | custom-call | tf_op jit(solution)/shard_map/sweep/pallas_call | solution.py:495
  71.9 1.7 %copy.7 = bf16[2,1,32,2048]{3,2,1,0:T(8,128)(2,1)} copy(bf16[2,1,32,2048]{3,2,1,0:T(8,128)(2,1)} %sweep.1) | data formatting | bytes 524288
